TPU v7x, 128 devices: a whole 4x4x4 slice. The times are simulated.
128 devices in a mesh: row: 8 (over x, y_hi), col: 16 (over y_lo, z, core).
Axes of the slice: x: 4, y: 4 (y_hi: 2, y_lo: 2; y = y_hi * 2 + y_lo), z: 4, core: 2. Of those that a mesh axis runs over, the one named last changes fastest.
Arguments:
- front_trailing: float32 [16384, 16384], P('row', 'col'), may hold values from -6 to 6
- panel_columns: float32 [16384, 1024], P('row', 'col'), may hold values from -0.1875 to 0.1875
- panel_rows: float32 [1024, 16384], P('row', 'col'), may hold values from -6 to 6
- pivots: int32 [1024], replicated, may hold values from 0 to 1023, each once
- diag_inverse: float32 [1024, 1024], replicated, may hold values from -0.1875 to 0.1875
- test_matrix: float32 [16384, 512], P('col'), may hold values from -0.046875 to 0.046875
Outputs:
- schur: float32 [16384, 16384], P('row', 'col')
- off_samples: float32 [16384, 512], P(('row', 'col'))
- leaf_blocks: float32 [16384, 128], P(('row', 'col'))
- group_gram: float32 [8, 512, 512], P('row')
Inputs may be any that keep to these rules, and one draw needn't show every extreme that they name: pivots names each of 0 to 1023 once.
All inputs are finite; a program needn't handle non-finite values.
Results may differ from a plain program's by a relative error of at most 0.000084.
Values sent between devices are 32-bit elements; how exact they have to be, the bound alone decides.
A program may use at most 128 MiB of HBM per device.

v0:
```python
import jax
import jax.numpy as jnp
from jax import lax
from jax.sharding import PartitionSpec as P

LEAF = 128


def product(left, right):
    return jnp.dot(left, right, precision=lax.Precision.HIGH, preferred_element_type=jnp.float32)


def body(front_trailing, panel_columns, panel_rows, pivots, diag_inverse, test_matrix):
    col_count = lax.axis_size("col")
    row_count = lax.axis_size("row")
    row_index = lax.axis_index("row")
    col_index = lax.axis_index("col")
    height, width = front_trailing.shape
    upper_full = lax.all_gather(panel_rows, "row", axis=0, tiled=True)
    left = lax.all_gather(panel_columns, "col", axis=1, tiled=True)
    upper = jnp.take(upper_full, pivots, axis=0)
    weight = product(diag_inverse, upper)
    schur = front_trailing - product(left, weight)
    rows = row_index * height + jnp.arange(height, dtype=jnp.int32)
    cols = col_index * width + jnp.arange(width, dtype=jnp.int32)
    same_leaf = rows[:, None] // LEAF == cols[None, :] // LEAF
    masked = jnp.where(same_leaf, jnp.zeros_like(schur), schur)
    partial = product(masked, test_matrix)
    count = width // LEAF
    ratio = col_count // row_count
    leaves = height // LEAF
    kept = []
    for leaf in range(leaves):
        held = col_index == row_index * ratio + leaf // count
        block = schur[
            leaf * LEAF : (leaf + 1) * LEAF, leaf % count * LEAF : (leaf % count + 1) * LEAF
        ]
        kept.append(jnp.where(held, block, jnp.zeros_like(block)))
    both = jnp.concatenate([partial, jnp.concatenate(kept, axis=0)], axis=1)
    own = lax.psum_scatter(both, "col", scatter_dimension=0, tiled=True)
    own_samples = own[:, : partial.shape[1]]
    leaf_blocks = own[:, partial.shape[1] :]
    gram = lax.dot_general(
        own_samples,
        own_samples,
        (((0,), (0,)), ((), ())),
        precision=lax.Precision.HIGH,
        preferred_element_type=jnp.float32,
    )
    gram = lax.psum(gram, "col")
    route = [(i, i ^ 1) for i in range(row_count)]
    gram = gram + lax.ppermute(gram, "row", route)
    group_gram = (gram / (2 * height))[None]
    return (schur, own_samples, leaf_blocks, group_gram)


def solution(mesh):
    placed = (P("row", "col"), P("row", "col"), P("row", "col"), P(), P(), P("col", None))
    return jax.shard_map(
        body,
        mesh=mesh,
        in_specs=placed,
        out_specs=(
            P("row", "col"),
            P(("row", "col"), None),
            P(("row", "col"), None),
            P("row", None, None),
        ),
        check_vma=False,
    )
```

profile of v0, /device:TPU:0, one launch (start us, length us, event | category | flops | bytes accessed | tf_op | source)
XLA Modules:
  0.0 392.7 jit_solution(6487991175751841340)
XLA Ops:
  7.2 0.0 copy-start
  7.2 0.0 all-gather.3.cloned.1.call-start
  7.2 0.7 all-gather.3.cloned.1.call-update
  7.9 0.0 all-gather.5.cloned.1.call-start
  8.0 0.7 all-gather.5.cloned.1.call-update
  8.7 0.0 reduce-scatter.2.cloned.1.call-start
  8.7 0.0 copy-start.3
  8.7 9.1 %copy.10 = f32[2048,1024]{0,1:T(8,128)} copy(f32[2048,1024]{1,0:T(8,128)} %param.6) | data formatting | bytes 16777216 | tf_op args[0]
  17.9 0.0 copy-done.3
  17.9 66.5 %all-gather.3.cloned.1.call-done = f32[1024,1024]{1,0:T(8,128)} async-done(((f32[128,1024]{1,0:T(8,128)}), f32[1024,1024]{1,0:T(8,128)}) %all-gather.3.cloned.1.call-update) | async-done | bytes 4194320 | tf_op jit(solution)/shard_map/all_gather | solution.py:19
  84.4 8.6 %gather_fusion = f32[1024,1024]{1,0:T(8,128)} fusion(f32[1024,1024]{1,0:T(8,128)} %all-gather.3.cloned.1.call-done, s32[1024]{0:T(1024)S(1)} %fusion.32), kind=kCustom, calls=%fused_computation | custom fusion | bytes 8392704 | tf_op jit(solution)/shard_map/jit(_take)/gather | solution.py:21
  93.0 17.9 %fusion.5 = f32[1024,1024]{1,0:T(8,128)} fusion(f32[1024,1024]{1,0:T(8,128)} %param.10, f32[1024,1024]{1,0:T(8,128)} %gather_fusion, pred[1024]{0:T(1024)(128)(4,1)S(1)} %compare_and_fusion), kind=kOutput, calls=%fused_computation.8 | convolution fusion | flops 6443499520 | bytes 12583936 | tf_op jit(solution)/shard_map/dot_general | solution.py:10
  110.9 25.2 %all-gather.5.cloned.1.call-done = f32[2048,1024]{0,1:T(8,128)} async-done(((f32[2048,64]{0,1:T(8,128)}), f32[2048,1024]{0,1:T(8,128)}) %all-gather.5.cloned.1.call-update) | async-done | bytes 8388624 | tf_op jit(solution)/shard_map/all_gather | solution.py:20
  136.1 17.8 %bitcast_subtract_fusion = f32[2048,1024]{0,1:T(8,128)S(1)} fusion(f32[2048,1024]{0,1:T(8,128)} %copy.10, f32[1024,1024]{1,0:T(8,128)} %fusion.5, f32[2048,1024]{0,1:T(8,128)} %all-gather.5.cloned.1.call-done), kind=kOutput, calls=%fused_computation.1 | convolution fusion | flops 12886999040 | bytes 29360128 | tf_op jit(solution)/shard_map/dot_general | solution.py:10
  154.0 0.0 copy-start.1
  154.3 0.0 copy-done
  154.3 7.6 %fusion = f32[2048,512]{0,1:T(8,128)S(1)} fusion(f32[1024,512]{1,0:T(8,128)S(1)} %copy-done, f32[2048,1024]{0,1:T(8,128)S(1)} %bitcast_subtract_fusion, s32[2048]{0:T(1024)S(1)} %add_select_fusion, s32[1024]{0:T(1024)S(1)} %add_select_fusion.1), kind=kOutput, calls=%fused_computation.2 | convolution fusion | flops 6446645248 | bytes 14692352 | tf_op jit(solution)/shard_map/dot_general | solution.py:10
  161.9 0.0 copy-done.1
  161.9 3.0 pad_maximum_fusion
  164.9 0.0 reduce-scatter.2.cloned.1.call-update
  164.9 0.0 all-reduce.2.cloned.1.call-start
  165.0 70.5 %reduce-scatter.2.cloned.1.call-done = f32[128,640]{0,1:T(8,128)} async-done(((f32[2048,640]{0,1:T(8,128)}), f32[128,640]{0,1:T(8,128)}) %reduce-scatter.2.cloned.1.call-update) | async-done | bytes 327696 | tf_op jit(solution)/shard_map/reduce_scatter | solution.py:40
  235.5 2.6 fusion.35
  238.1 0.0 all-reduce.2.cloned.1.call-update
  238.1 0.0 slice-start
  238.1 0.0 slice-start.1
  238.1 119.0 %all-reduce.2.cloned.1.call-done = f32[512,512]{1,0:T(8,128)} async-done(((f32[512,512]{1,0:T(8,128)}), f32[512,512]{1,0:T(8,128)}) %all-reduce.2.cloned.1.call-update) | async-done | bytes 1048592 | tf_op jit(solution)/shard_map/psum | solution.py:50
  357.1 0.0 copy-start.2
  357.1 2.7 collective-permute-start
  359.8 9.2 %copy.11 = f32[2048,1024]{1,0:T(8,128)} copy(f32[2048,1024]{0,1:T(8,128)} %copy-done.1) | data formatting | bytes 16777216
  369.1 0.0 slice-done
  369.1 0.8 copy.12
  369.9 0.0 slice-done.1
  369.9 0.7 copy.13
  370.6 13.1 %collective-permute-done = f32[512,512]{1,0:T(8,128)} collective-permute-done((f32[512,512]{1,0:T(8,128)}, f32[512,512]{1,0:T(8,128)}, u32[]{:S(2)}, u32[]{:S(2)}) %collective-permute-start) | collective-permute-done | bytes 1048608 | tf_op jit(solution)/shard_map/ppermute | solution.py:52
  383.7 0.0 copy-done.2
  383.7 2.4 multiply_bitcast_fusion
  (20 shorter events, 0.2 us)
Async XLA Ops:
  7.2 147.1 %copy-start = (f32[1024,512]{1,0:T(8,128)S(1)}, f32[1024,512]{1,0:T(8,128)}, u32[]{:S(2)}) copy-start(f32[1024,512]{1,0:T(8,128)} %param.11) | copy-start | bytes 6291460
  7.2 77.2 %all-gather.3.cloned.1.call-start = ((), (), s32[]{:S(2)}) async-start(), calls=%async_computation.1 | async-start | bytes 4718592 | tf_op jit(solution)/shard_map/all_gather | solution.py:19
  7.9 128.2 %all-gather.5.cloned.1.call-start = ((), (), s32[]{:S(2)}) async-start(), calls=%async_computation.2 | async-start | bytes 8912896 | tf_op jit(solution)/shard_map/all_gather | solution.py:20
  8.7 226.8 %reduce-scatter.2.cloned.1.call-start = ((), (), s32[]{:S(2)}) async-start(), calls=%async_computation.3 | async-start | bytes 5570560 | tf_op jit(solution)/shard_map/reduce_scatter | solution.py:40
  8.7 9.2 %copy-start.3 = (s32[1024]{0:T(1024)S(1)}, s32[1024]{0:T(1024)}, u32[]{:S(2)}) copy-start(s32[1024]{0:T(1024)} %param.9) | copy-start | bytes 12292
  154.0 7.9 %copy-start.1 = (f32[2048,1024]{0,1:T(8,128)}, f32[2048,1024]{0,1:T(8,128)S(1)}, u32[]{:S(2)}) copy-start(f32[2048,1024]{0,1:T(8,128)S(1)} %bitcast_subtract_fusion) | copy-start | bytes 25165828
  164.9 192.2 %all-reduce.2.cloned.1.call-start = ((), (), s32[]{:S(2)}) async-start(), calls=%async_computation.4 | async-start | bytes 2097152 | tf_op jit(solution)/shard_map/psum | solution.py:50
  238.1 131.0 %slice-start = ((f32[128,640]{0,1:T(8,128)}), f32[128,512]{0,1:T(8,128)S(1)}, s32[]{:S(2)}) async-start(f32[128,640]{0,1:T(8,128)} %reduce-scatter.2.cloned.1.call-done), calls=%async_computation.5 | async-start | bytes 524288 | tf_op jit(solution)/shard_map/slice | solution.py:41
  238.1 131.8 %slice-start.1 = ((f32[128,640]{0,1:T(8,128)}), f32[128,128]{0,1:T(8,128)S(1)}, s32[]{:S(2)}) async-start(f32[128,640]{0,1:T(8,128)} %reduce-scatter.2.cloned.1.call-done), calls=%async_computation.6 | async-start | bytes 131072 | tf_op jit(solution)/shard_map/slice | solution.py:42
  357.1 26.6 %copy-start.2 = (f32[512,512]{1,0:T(8,128)S(1)}, f32[512,512]{1,0:T(8,128)}, u32[]{:S(2)}) copy-start(f32[512,512]{1,0:T(8,128)} %all-reduce.2.cloned.1.call-done) | copy-start | bytes 3145732
  357.1 26.6 %collective-permute-start = (f32[512,512]{1,0:T(8,128)}, f32[512,512]{1,0:T(8,128)}, u32[]{:S(2)}, u32[]{:S(2)}) collective-permute-start(f32[512,512]{1,0:T(8,128)} %all-reduce.2.cloned.1.call-done), channel_id=1, source_target_pairs={{0,16},{16,0},{32,48},{48,32},{64,80},{80,64},{96,112},{112,96},{1... | collective-permute-start | bytes 3145736 | tf_op jit(solution)/shard_map/ppermute | solution.py:52
Sparse Core Ops, SparseCore 0:
  10.3 74.0 all-gather.2
  86.1 49.9 all-gather.4
  165.0 70.3 reduce-scatter.1
  238.4 118.7 all-reduce.1
where the time goes:
time: 393 us
  waiting for transfers between devices  296 us (75%)
  matrix products  45.9 us (12%)
  local copies, waits for them, and re-layouts  28.6 us (7%)
  between operations  14 us (4%)
  other arithmetic  5.64 us (1%)
    psum x1, waiting for transfers between devices, body(): gram = lax.psum(gram, 'col')  119 us
    reduce_scatter x1, waiting for transfers between devices, body(): own = lax.psum_scatter(both, 'col', scatter_dimension=0, tiled=True)  70.5 us
    all_gather x1, waiting for transfers between devices, body(): upper_full = lax.all_gather(panel_rows, 'row', axis=0, tiled=True)  66.5 us
    dot_general x3, matrix products, product(): jnp.dot(left, right, precision=lax.Precision.HIGH, preferred_element_type...  43.3 us
    all_gather x1, waiting for transfers between devices, body(): left = lax.all_gather(panel_columns, 'col', axis=1, tiled=True)  25.2 us
    unnamed x12, local copies, waits for them, and re-layouts  20 us
    ppermute x1, waiting for transfers between devices, body(): gram = gram + lax.ppermute(gram, 'row', route)  13.1 us
    gather x1, local copies, waits for them, and re-layouts, body(): upper = jnp.take(upper_full, pivots, axis=0)  8.63 us
  transfers between devices with their start and end apart: 5, of which 5 were waited for; matrix products, arithmetic and copies ran while one was open for 12% of the time, Pallas kernels for 0%

commit v1 on v0

--- a/solution.py
+++ b/solution.py
@@ -47,7 +47,7 @@
         precision=lax.Precision.HIGH,
         preferred_element_type=jnp.float32,
     )
-    gram = lax.psum(gram, "col")
+    gram = jnp.sum(lax.all_gather(gram, "col"), axis=0)
     route = [(i, i ^ 1) for i in range(row_count)]
     gram = gram + lax.ppermute(gram, "row", route)
     group_gram = (gram / (2 * height))[None]

time: 393 us -> 373 us (0.949)
  waiting for transfers between devices: 296 us -> 267 us
  other arithmetic: 5.64 us -> 13.6 us
    psum x1 -> x0, waiting for transfers between devices: 119 us -> none  [body(): gram = lax.psum(gram, 'col')]
    all_gather x0 -> x1, waiting for transfers between devices: none -> 90.1 us  [body(): gram = jnp.sum(lax.all_gather(gram, 'col'), axis=0)]
    reduce_sum x0 -> x1, other arithmetic: none -> 7.91 us  [body(): gram = jnp.sum(lax.all_gather(gram, 'col'), axis=0)]
    unnamed x12 -> x10, local copies, waits for them, and re-layouts: 20 us -> 20 us
where the time goes in v1:
time: 373 us; the launch traced here: 372 us
  waiting for transfers between devices  267 us (72%)
  matrix products  45.9 us (12%)
  local copies, waits for them, and re-layouts  28.6 us (8%)
  between operations  14 us (4%)
  other arithmetic  13.6 us (4%)
    all_gather x1, waiting for transfers between devices, body(): gram = jnp.sum(lax.all_gather(gram, 'col'), axis=0)  90.1 us
    reduce_scatter x1, waiting for transfers between devices, body(): own = lax.psum_scatter(both, 'col', scatter_dimension=0, tiled=True)  70.5 us
    all_gather x1, waiting for transfers between devices, body(): upper_full = lax.all_gather(panel_rows, 'row', axis=0, tiled=True)  66.5 us
    dot_general x3, matrix products, product(): jnp.dot(left, right, precision=lax.Precision.HIGH, preferred_element_type...  43.3 us
    all_gather x1, waiting for transfers between devices, body(): left = lax.all_gather(panel_columns, 'col', axis=1, tiled=True)  25.2 us
    unnamed x10, local copies, waits for them, and re-layouts  20 us
    ppermute x1, waiting for transfers between devices, body(): gram = gram + lax.ppermute(gram, 'row', route)  13.1 us
    gather x1, local copies, waits for them, and re-layouts, body(): upper = jnp.take(upper_full, pivots, axis=0)  8.59 us
  transfers between devices with their start and end apart: 5, of which 5 were waited for; matrix products, arithmetic and copies ran while one was open for 12% of the time, Pallas kernels for 0%

profile of v1, /device:TPU:0, one launch (start us, length us, event | category | flops | bytes accessed | tf_op | source)
XLA Modules:
  0.0 372.1 jit_solution(11364131797273274324)
XLA Ops:
  7.2 0.0 copy-start
  7.2 0.0 all-gather.5.cloned.1.call-start
  7.2 0.7 all-gather.5.cloned.1.call-update
  7.9 0.0 all-gather.7.cloned.1.call-start
  8.0 0.7 all-gather.7.cloned.1.call-update
  8.7 0.0 reduce-scatter.2.cloned.1.call-start
  8.7 0.0 copy-start.2
  8.7 9.1 %copy.10 = f32[2048,1024]{0,1:T(8,128)} copy(f32[2048,1024]{1,0:T(8,128)} %param.6) | data formatting | bytes 16777216 | tf_op args[0]
  17.9 0.0 copy-done.2
  17.9 66.5 %all-gather.5.cloned.1.call-done = f32[1024,1024]{1,0:T(8,128)} async-done(((f32[128,1024]{1,0:T(8,128)}), f32[1024,1024]{1,0:T(8,128)}) %all-gather.5.cloned.1.call-update) | async-done | bytes 4194320 | tf_op jit(solution)/shard_map/all_gather | solution.py:19
  84.4 8.6 %gather_fusion = f32[1024,1024]{1,0:T(8,128)} fusion(f32[1024,1024]{1,0:T(8,128)} %all-gather.5.cloned.1.call-done, s32[1024]{0:T(1024)S(1)} %fusion.32), kind=kCustom, calls=%fused_computation | custom fusion | bytes 8392704 | tf_op jit(solution)/shard_map/jit(_take)/gather | solution.py:21
  93.0 17.9 %fusion.5 = f32[1024,1024]{1,0:T(8,128)} fusion(f32[1024,1024]{1,0:T(8,128)} %param.10, f32[1024,1024]{1,0:T(8,128)} %gather_fusion, pred[1024]{0:T(1024)(128)(4,1)S(1)} %compare_and_fusion), kind=kOutput, calls=%fused_computation.8 | convolution fusion | flops 6443499520 | bytes 12583936 | tf_op jit(solution)/shard_map/dot_general | solution.py:10
  110.9 25.2 %all-gather.7.cloned.1.call-done = f32[2048,1024]{0,1:T(8,128)} async-done(((f32[2048,64]{0,1:T(8,128)}), f32[2048,1024]{0,1:T(8,128)}) %all-gather.7.cloned.1.call-update) | async-done | bytes 8388624 | tf_op jit(solution)/shard_map/all_gather | solution.py:20
  136.1 17.8 %bitcast_subtract_fusion = f32[2048,1024]{0,1:T(8,128)S(1)} fusion(f32[2048,1024]{0,1:T(8,128)} %copy.10, f32[1024,1024]{1,0:T(8,128)} %fusion.5, f32[2048,1024]{0,1:T(8,128)} %all-gather.7.cloned.1.call-done), kind=kOutput, calls=%fused_computation.1 | convolution fusion | flops 12886999040 | bytes 29360128 | tf_op jit(solution)/shard_map/dot_general | solution.py:10
  154.0 0.0 copy-start.1
  154.3 0.0 copy-done
  154.3 7.6 %fusion = f32[2048,512]{0,1:T(8,128)S(1)} fusion(f32[1024,512]{1,0:T(8,128)S(1)} %copy-done, f32[2048,1024]{0,1:T(8,128)S(1)} %bitcast_subtract_fusion, s32[2048]{0:T(1024)S(1)} %add_select_fusion, s32[1024]{0:T(1024)S(1)} %add_select_fusion.1), kind=kOutput, calls=%fused_computation.2 | convolution fusion | flops 6446645248 | bytes 14692352 | tf_op jit(solution)/shard_map/dot_general | solution.py:10
  161.9 0.0 copy-done.1
  161.9 3.0 pad_maximum_fusion
  164.9 0.0 reduce-scatter.2.cloned.1.call-update
  164.9 0.0 all-gather.9.cloned.1.call-start
  165.0 70.5 %reduce-scatter.2.cloned.1.call-done = f32[128,640]{0,1:T(8,128)} async-done(((f32[2048,640]{0,1:T(8,128)}), f32[128,640]{0,1:T(8,128)}) %reduce-scatter.2.cloned.1.call-update) | async-done | bytes 327696 | tf_op jit(solution)/shard_map/reduce_scatter | solution.py:40
  235.5 2.6 fusion.35
  238.0 0.0 all-gather.9.cloned.1.call-update
  238.1 90.1 %all-gather.9.cloned.1.call-done = f32[8192,512]{1,0:T(8,128)} async-done(((f32[512,512]{1,0:T(8,128)}), f32[8192,512]{1,0:T(8,128)}) %all-gather.9.cloned.1.call-update) | async-done | bytes 16777232 | tf_op jit(solution)/shard_map/all_gather | solution.py:50
  328.2 7.9 %reduce_sum.9 = f32[512,512]{1,0:T(8,128)S(1)} reduce(f32[16,512,512]{2,1,0:T(8,128)} %bitcast.9, f32[]{:T(128)} %constant.59.clone.1), dimensions={0}, to_apply=%region_1.2 | reduce | flops 3932160 | bytes 17825796 | tf_op jit(solution)/shard_map/reduce_sum | solution.py:50
  336.1 0.0 slice-start
  336.1 0.0 slice-start.1
  336.1 3.1 collective-permute-start
  339.2 9.2 %copy.11 = f32[2048,1024]{1,0:T(8,128)} copy(f32[2048,1024]{0,1:T(8,128)} %copy-done.1) | data formatting | bytes 16777216
  348.5 0.0 slice-done
  348.5 0.7 copy.13
  349.2 0.0 slice-done.1
  349.2 0.8 copy.12
  350.0 13.1 %collective-permute-done = f32[512,512]{1,0:T(8,128)} collective-permute-done((f32[512,512]{1,0:T(8,128)S(1)}, f32[512,512]{1,0:T(8,128)}, u32[]{:S(2)}, u32[]{:S(2)}) %collective-permute-start) | collective-permute-done | bytes 1048608 | tf_op jit(solution)/shard_map/ppermute | solution.py:52
  363.1 2.4 multiply_bitcast_fusion
  (20 shorter events, 0.2 us)
Async XLA Ops:
  7.2 147.1 %copy-start = (f32[1024,512]{1,0:T(8,128)S(1)}, f32[1024,512]{1,0:T(8,128)}, u32[]{:S(2)}) copy-start(f32[1024,512]{1,0:T(8,128)} %param.11) | copy-start | bytes 6291460
  7.2 77.2 %all-gather.5.cloned.1.call-start = ((), (), s32[]{:S(2)}) async-start(), calls=%async_computation.1 | async-start | bytes 4718592 | tf_op jit(solution)/shard_map/all_gather | solution.py:19
  7.9 128.2 %all-gather.7.cloned.1.call-start = ((), (), s32[]{:S(2)}) async-start(), calls=%async_computation.2 | async-start | bytes 8912896 | tf_op jit(solution)/shard_map/all_gather | solution.py:20
  8.7 226.8 %reduce-scatter.2.cloned.1.call-start = ((), (), s32[]{:S(2)}) async-start(), calls=%async_computation.3 | async-start | bytes 5570560 | tf_op jit(solution)/shard_map/reduce_scatter | solution.py:40
  8.7 9.2 %copy-start.2 = (s32[1024]{0:T(1024)S(1)}, s32[1024]{0:T(1024)}, u32[]{:S(2)}) copy-start(s32[1024]{0:T(1024)} %param.9) | copy-start | bytes 12292
  154.0 7.9 %copy-start.1 = (f32[2048,1024]{0,1:T(8,128)}, f32[2048,1024]{0,1:T(8,128)S(1)}, u32[]{:S(2)}) copy-start(f32[2048,1024]{0,1:T(8,128)S(1)} %bitcast_subtract_fusion) | copy-start | bytes 25165828
  164.9 163.3 %all-gather.9.cloned.1.call-start = ((), (), s32[]{:S(2)}) async-start(), calls=%async_computation.4 | async-start | bytes 17825792 | tf_op jit(solution)/shard_map/all_gather | solution.py:50
  336.1 12.4 %slice-start = ((f32[128,640]{0,1:T(8,128)}), f32[128,128]{0,1:T(8,128)S(1)}, s32[]{:S(2)}) async-start(f32[128,640]{0,1:T(8,128)} %reduce-scatter.2.cloned.1.call-done), calls=%async_computation.5 | async-start | bytes 131072 | tf_op jit(solution)/shard_map/slice | solution.py:42
  336.1 13.1 %slice-start.1 = ((f32[128,640]{0,1:T(8,128)}), f32[128,512]{0,1:T(8,128)S(1)}, s32[]{:S(2)}) async-start(f32[128,640]{0,1:T(8,128)} %reduce-scatter.2.cloned.1.call-done), calls=%async_computation.6 | async-start | bytes 524288 | tf_op jit(solution)/shard_map/slice | solution.py:41
  336.1 27.0 %collective-permute-start = (f32[512,512]{1,0:T(8,128)S(1)}, f32[512,512]{1,0:T(8,128)}, u32[]{:S(2)}, u32[]{:S(2)}) collective-permute-start(f32[512,512]{1,0:T(8,128)S(1)} %reduce_sum.9), channel_id=1, source_target_pairs={{0,16},{16,0},{32,48},{48,32},{64,80},{80,64},{96,112},{112,96},{1... | collective-permute-start | bytes 3145736 | tf_op jit(solution)/shard_map/ppermute | solution.py:52
Sparse Core Ops, SparseCore 0:
  10.3 74.0 all-gather.4
  86.1 49.9 all-gather.6
  165.0 70.3 reduce-scatter.1
  238.2 89.9 all-gather.8
